TPU v7x, 32 devices: a whole 2x2x4 slice. The times are simulated.
32 devices in a mesh: obs: 4 (over z), src: 8 (over y, x, core).
Axes of the slice: x: 2, y: 2, z: 4, core: 2. Of those that a mesh axis runs over, the one named last changes fastest.
Arguments:
- history: bfloat16 [3, 64, 64, 1536], P(None, ('obs', 'src')), may hold values from -6 to 6
- incident: bfloat16 [5, 64, 64, 1536], P(None, ('obs', 'src')), may hold values from -6 to 6
- proj_basis: bfloat16 [64, 64, 1536], P(('obs', 'src')), may hold values from -0.15625 to 0.15625
- expand_basis: bfloat16 [64, 64, 1536], P(('obs', 'src')), may hold values from -0.75 to 0.75
- near_inverse: bfloat16 [64, 1536, 1536], P(('obs', 'src')), may hold values from -0.15625 to 0.15625
- couplings: bfloat16 [2, 4096, 4, 8, 128], P(None, 'obs', None, 'src'), may hold values from -0.09375 to 0.09375
- lags: int32 [64, 4, 8, 2], P('obs', None, 'src'), may hold values from 0 to 2, as said below
Outputs:
- currents: bfloat16 [5, 64, 64, 1536], P(None, ('obs', 'src'))
Inputs may be any that keep to these rules, and one draw needn't show every extreme that they name: lags[j, o, s, k] is the lag from source cluster j to observer cluster (o * 8 + s) * 2 + k. Entries are 0, 1 or 2, and the entry of every cluster with itself is 0.
All inputs are finite; a program needn't handle non-finite values.
Results may differ from a plain program's by a relative error of at most 0.025.
Values may be sent and summed in bfloat16 or wider, within the bound.
A program may use at most 192 MiB of HBM per device.

v0:
```python
import jax
import jax.numpy as jnp
from jax import lax
from jax.sharding import PartitionSpec as P

STEPS = 5
TAPS = 2
HIST = 3


def per_device(history, incident, proj_basis, expand_basis, near_inverse, couplings, lags):
    rank = proj_basis.shape[1]
    local_clusters = proj_basis.shape[0]
    excite = history.shape[2]
    src_rows = couplings.shape[1]
    obs_cols = couplings.shape[2] * couplings.shape[3] * couplings.shape[4]
    src_clusters = lags.shape[0]
    obs_clusters = lags.shape[1] * lags.shape[2] * lags.shape[3]
    kernel = couplings.reshape(TAPS, src_clusters, rank, obs_clusters, rank)
    lag_pairs = lags.reshape(src_clusters, obs_clusters)
    matrices = []
    for delay in range(1, HIST + 1):
        combined = jnp.zeros_like(kernel[0])
        for tap_index in range(TAPS):
            if delay - tap_index >= 1:
                chosen = (lag_pairs == delay - tap_index)[:, None, :, None]
                combined = jnp.where(chosen, kernel[tap_index], combined)
        matrices.append(combined.reshape(src_rows, obs_cols))

    def project(current):
        projected = jnp.einsum(
            "ceb,crb->ecr", current, proj_basis, preferred_element_type=jnp.float32
        )
        return projected.astype(jnp.bfloat16).reshape(excite, local_clusters * rank)

    def couple(columns, delay):
        return jnp.dot(columns, matrices[delay - 1], preferred_element_type=jnp.float32)

    stacked = jnp.stack([project(history[slot_index]) for slot_index in range(HIST)])
    gathered = lax.all_gather(stacked, "src", axis=2, tiled=True)
    past = [gathered[slot_index] for slot_index in range(HIST)]
    results = []
    latest = None
    for step in range(STEPS):
        if step > 0:
            newest = lax.all_gather(latest, "src", axis=1, tiled=True)
            past = past[1:] + [newest]
        partial_value = couple(past[-1], 1) + couple(past[-2], 2) + couple(past[-3], 3)
        field = lax.psum_scatter(
            partial_value.astype(jnp.bfloat16), "obs", scatter_dimension=1, tiled=True
        )
        field_cast = field.reshape(excite, local_clusters, rank)
        far_field = jnp.einsum(
            "ecr,crb->ceb", field_cast, expand_basis, preferred_element_type=jnp.float32
        )
        residual_field = (incident[step].astype(jnp.float32) - far_field).astype(jnp.bfloat16)
        current = jnp.einsum(
            "ceb,cbd->ced", residual_field, near_inverse, preferred_element_type=jnp.float32
        ).astype(jnp.bfloat16)
        results.append(current)
        if step + 1 < STEPS:
            latest = project(current)
    return jnp.stack(results)


def solution(mesh):
    placed = (
        P(None, ("obs", "src"), None, None),
        P(None, ("obs", "src"), None, None),
        P(("obs", "src"), None, None),
        P(("obs", "src"), None, None),
        P(("obs", "src"), None, None),
        P(None, "obs", None, "src", None),
        P("obs", None, "src", None),
    )
    return jax.shard_map(
        per_device,
        mesh=mesh,
        in_specs=placed,
        out_specs=P(None, ("obs", "src"), None, None),
        check_vma=False,
    )
```

profile of v0, /device:TPU:0, one launch (start us, length us, event | category | flops | bytes accessed | tf_op | source)
XLA Modules:
  0.0 237.1 jit_solution(1757093044412803134)
XLA Ops:
  6.5 1.4 convolution_convert_fusion.11
  8.0 1.4 convolution_convert_fusion.10
  9.3 1.4 convolution_convert_fusion.9
  11.1 2.3 fusion.46
  13.3 2.0 squeeze.40
  15.3 1.8 squeeze.42
  17.2 4.3 %select_select_fusion = (bf16[16,64,8,64]{3,2,1,0:T(8,128)(2,1)}, bf16[16,64,8,64]{3,2,1,0:T(8,128)(2,1)}, bf16[16,64,8,64]{3,2,1,0:T(8,128)(2,1)}) fusion(bf16[16,64,8,64]{3,2,1,0:T(8,128)(2,1)} %squeeze.42, bf16[16,64,8,64]{3,2,1,0:T(8,128)(2,1)} %squeeze.40, pred[16,8]{1,0:T(8,128)(4,1)S(1)} %copy.20, pred[16,8]{1,0:T(8,128)(4,1)S(1)} %copy.19, ...), kind=kLoop, calls=%fused_computation.17 | loop fusion | flops 2621440 | bytes 5243264 | tf_op jit(solution)/shard_map/jit(_where)/select_n | solution.py:27
  21.5 4.0 %select_n.97 = bf16[1024,512]{1,0:T(8,128)(2,1)} reshape(bf16[16,64,8,64]{3,2,1,0:T(8,128)(2,1)} %get-tuple-element.7) | data formatting | bytes 2097152 | tf_op jit(solution)/shard_map/jit(_where)/select_n | solution.py:27
  25.6 11.9 %all_gather.15 = bf16[3,64,1024]{1,2,0:T(8,128)(2,1)S(1)} all-gather(bf16[3,64,128]{1,2,0:T(8,128)(2,1)S(1)} %pad_maximum_fusion), channel_id=1, replica_groups=mesh['obs'=4,'src'=8] {'src'}, dimensions={2}, use_global_device_ids=true | all-gather | bytes 442368 | tf_op jit(solution)/shard_map/all_gather | solution.py:40
  37.5 3.5 %select_n.100 = bf16[1024,512]{1,0:T(8,128)(2,1)S(1)} reshape(bf16[16,64,8,64]{3,2,1,0:T(8,128)(2,1)} %get-tuple-element.6) | data formatting | bytes 2097152 | tf_op jit(solution)/shard_map/jit(_where)/select_n | solution.py:27
  41.0 3.2 %select_n.103 = bf16[1024,512]{1,0:T(8,128)(2,1)S(1)} reshape(bf16[16,64,8,64]{3,2,1,0:T(8,128)(2,1)} %get-tuple-element.5) | data formatting | bytes 2097152 | tf_op jit(solution)/shard_map/jit(_where)/select_n | solution.py:27
  44.2 1.5 fusion.42
  47.2 1.0 fusion.39
  48.5 2.7 %broadcast_in_dim.38 = pred[1024,512]{1,0:T(32,128)(4,1)} reshape(pred[16,64,8,64]{3,2,1,0:T(8,128)(4,1)S(1)} %broadcast_in_dim.35) | data formatting | bytes 1048576 | tf_op jit(solution)/shard_map/jit(_where)/broadcast_in_dim | solution.py:27
  51.6 2.7 %broadcast_in_dim.39 = pred[1024,512]{1,0:T(32,128)(4,1)} reshape(pred[16,64,8,64]{3,2,1,0:T(8,128)(4,1)S(1)} %broadcast_in_dim.36) | data formatting | bytes 1048576 | tf_op jit(solution)/shard_map/jit(_where)/broadcast_in_dim | solution.py:27
  54.3 2.5 %bitcast_select_fusion.1 = bf16[1024,512]{1,0:T(8,128)(2,1)S(1)} fusion(pred[1024,512]{1,0:T(32,128)(4,1)} %broadcast_in_dim.38, pred[1024,512]{1,0:T(32,128)(4,1)} %broadcast_in_dim.39, bf16[128,8,4,128]{3,2,1,0:T(4,128)(2,1)} %bitcast.199, bf16[128,8,4,128]{3,2,1,0:T(4,128)(2,1)} %bitcast.202), kind=kLoop, calls=%fused_computation.47 | loop fusion | flops 1048576 | bytes 4194304 | tf_op jit(solution)/shard_map/jit(_where)/select_n | solution.py:27
  56.8 1.9 fusion.41
  58.8 8.2 %reduce-scatter.16.cloned.1.call-done = bf16[128,64]{1,0:T(8,128)(2,1)} async-done(((bf16[512,64]{1,0:T(8,128)(2,1)}), bf16[128,64]{1,0:T(8,128)(2,1)}) %reduce-scatter.16.cloned.1.call-update) | async-done | bytes 16400
  67.0 6.7 %bitcast_dynamic-update-slice_fusion.3 = (bf16[5,2,64,1536]{3,2,1,0:T(8,128)(2,1)}, bf16[2,64,1536]{2,1,0:T(8,128)(2,1)}) fusion(bf16[2,1536,1536]{2,1,0:T(8,128)(2,1)} %param.11, bf16[64,2,64]{0,2,1:T(8,128)(2,1)} %bitcast.214, bf16[2,64,1536]{2,1,0:T(8,128)(2,1)S(1)} %copy-done, bf16[5,2,64,1536]{3,2,1,0:T(8,128)(2,1)} %param.8), kind=kOutput, calls=%fused_computation.64 | convolution fusion | flops 629932032 | bytes 11042816 | tf_op jit(solution)/shard_map/ceb,cbd->ced/dot_general | solution.py:57
  73.8 1.4 fusion.14
  75.8 0.8 reshape.176
  76.6 9.2 %all_gather.16 = bf16[64,1024]{1,0:T(8,128)(2,1)S(1)} all-gather(bf16[64,128]{1,0:T(8,128)(2,1)S(1)} %reshape.176), channel_id=1, replica_groups=mesh['obs'=4,'src'=8] {'src'}, dimensions={1}, use_global_device_ids=true | all-gather | bytes 147456 | tf_op jit(solution)/shard_map/all_gather | solution.py:46
  86.5 2.3 fusion.13
  88.7 1.6 copy.32
  90.4 1.9 fusion.40
  92.3 14.9 %reduce-scatter.18.cloned.1.call-done = bf16[128,64]{1,0:T(8,128)(2,1)} async-done(((bf16[512,64]{1,0:T(8,128)(2,1)}), bf16[128,64]{1,0:T(8,128)(2,1)}) %reduce-scatter.18.cloned.1.call-update) | async-done | bytes 16400
  107.2 6.7 %bitcast_dynamic-update-slice_fusion.2 = (bf16[5,2,64,1536]{3,2,1,0:T(8,128)(2,1)}, bf16[2,64,1536]{2,1,0:T(8,128)(2,1)}) fusion(bf16[5,2,64,1536]{3,2,1,0:T(8,128)(2,1)} %get-tuple-element.13, bf16[2,1536,1536]{2,1,0:T(8,128)(2,1)} %param.11, bf16[64,2,64]{0,2,1:T(8,128)(2,1)} %bitcast.216, bf16[2,64,1536]{2,1,0:T(8,128)(2,1)S(1)} %copy-done, ...), kind=kOutput, calls=%fused_computation.63 | convolution fusion | flops 629932032 | bytes 11042816 | tf_op jit(solution)/shard_map/ceb,cbd->ced/dot_general | solution.py:57
  114.0 1.3 fusion.15
  115.9 0.8 reshape.178
  116.7 9.1 %all_gather.17 = bf16[64,1024]{1,0:T(8,128)(2,1)S(1)} all-gather(bf16[64,128]{1,0:T(8,128)(2,1)S(1)} %reshape.178), channel_id=1, replica_groups=mesh['obs'=4,'src'=8] {'src'}, dimensions={1}, use_global_device_ids=true | all-gather | bytes 147456 | tf_op jit(solution)/shard_map/all_gather | solution.py:46
  127.7 1.3 broadcast_in_dim.37
  129.0 4.0 %broadcast_in_dim.40 = pred[1024,512]{1,0:T(32,128)(4,1)} reshape(pred[16,64,8,64]{3,2,1,0:T(8,128)(4,1)} %broadcast_in_dim.37) | data formatting | bytes 1048576 | tf_op jit(solution)/shard_map/jit(_where)/broadcast_in_dim | solution.py:27
  133.0 11.5 %reduce-scatter.20.cloned.1.call-done = bf16[128,64]{1,0:T(8,128)(2,1)} async-done(((bf16[512,64]{1,0:T(8,128)(2,1)}), bf16[128,64]{1,0:T(8,128)(2,1)}) %reduce-scatter.20.cloned.1.call-update) | async-done | bytes 16400
  144.5 6.6 %bitcast_dynamic-update-slice_fusion.1 = (bf16[5,2,64,1536]{3,2,1,0:T(8,128)(2,1)}, bf16[2,64,1536]{2,1,0:T(8,128)(2,1)S(1)}) fusion(bf16[5,2,64,1536]{3,2,1,0:T(8,128)(2,1)} %get-tuple-element.15, bf16[2,1536,1536]{2,1,0:T(8,128)(2,1)} %param.11, bf16[64,2,64]{0,2,1:T(8,128)(2,1)} %bitcast.215, bf16[2,64,1536]{2,1,0:T(8,128)(2,1)S(1)} %copy-done, ...), kind=kOutput, calls=%fused_computation.62 | convolution fusion | flops 629932032 | bytes 11042816 | tf_op jit(solution)/shard_map/ceb,cbd->ced/dot_general | solution.py:57
  152.0 0.9 reshape.180
  152.9 9.1 %all_gather.18 = bf16[64,1024]{1,0:T(8,128)(2,1)S(1)} all-gather(bf16[64,128]{1,0:T(8,128)(2,1)S(1)} %reshape.180), channel_id=1, replica_groups=mesh['obs'=4,'src'=8] {'src'}, dimensions={1}, use_global_device_ids=true | all-gather | bytes 147456 | tf_op jit(solution)/shard_map/all_gather | solution.py:46
  162.7 1.6 fusion.44
  164.7 1.5 fusion.9
  166.1 1.6 copy.36
  167.8 16.8 %reduce-scatter.22.cloned.1.call-done = bf16[128,64]{1,0:T(8,128)(2,1)} async-done(((bf16[512,64]{1,0:T(8,128)(2,1)}), bf16[128,64]{1,0:T(8,128)(2,1)}) %reduce-scatter.22.cloned.1.call-update) | async-done | bytes 16400
  184.6 6.7 %bitcast_dynamic-update-slice_fusion = (bf16[5,2,64,1536]{3,2,1,0:T(8,128)(2,1)}, bf16[2,64,1536]{2,1,0:T(8,128)(2,1)}) fusion(bf16[5,2,64,1536]{3,2,1,0:T(8,128)(2,1)} %get-tuple-element.17, bf16[2,1536,1536]{2,1,0:T(8,128)(2,1)} %param.11, bf16[64,2,64]{0,2,1:T(8,128)(2,1)} %bitcast.217, bf16[2,64,1536]{2,1,0:T(8,128)(2,1)S(1)} %copy-done, ...), kind=kOutput, calls=%fused_computation.61 | convolution fusion | flops 629932032 | bytes 11042816 | tf_op jit(solution)/shard_map/ceb,cbd->ced/dot_general | solution.py:57
  191.3 1.4 fusion.17
  193.3 0.8 reshape.182
  194.2 9.4 %all_gather.19 = bf16[64,1024]{1,0:T(8,128)(2,1)S(1)} all-gather(bf16[64,128]{1,0:T(8,128)(2,1)S(1)} %reshape.182), channel_id=1, replica_groups=mesh['obs'=4,'src'=8] {'src'}, dimensions={1}, use_global_device_ids=true | all-gather | bytes 147456 | tf_op jit(solution)/shard_map/all_gather | solution.py:46
  203.6 1.6 fusion.43
  205.5 0.8 fusion.10
  207.1 16.9 %reduce-scatter.24.cloned.1.call-done = bf16[128,64]{1,0:T(8,128)(2,1)} async-done(((bf16[512,64]{1,0:T(8,128)(2,1)}), bf16[128,64]{1,0:T(8,128)(2,1)}) %reduce-scatter.24.cloned.1.call-update) | async-done | bytes 16400
  224.0 6.6 %fusion.6 = bf16[5,2,64,1536]{3,2,1,0:T(8,128)(2,1)} fusion(bf16[5,2,64,1536]{3,2,1,0:T(8,128)(2,1)} %get-tuple-element.19, bf16[2,1536,1536]{2,1,0:T(8,128)(2,1)} %param.11, bf16[64,2,64]{0,2,1:T(8,128)(2,1)} %bitcast.218, bf16[2,64,1536]{2,1,0:T(8,128)(2,1)S(1)} %copy-done, bf16[5,2,64,1536]{3,2,1,0:T(8,128)(2,1)} %param.8), kind=kOutput, calls=%fused_computation.16 | convolution fusion | flops 629932032 | bytes 10649600 | tf_op jit(solution)/shard_map/ceb,cbd->ced/dot_general | solution.py:57
  (82 shorter events, 9.9 us)
Async XLA Ops:
  6.5 60.5 %copy-start = (bf16[2,64,1536]{2,1,0:T(8,128)(2,1)S(1)}, bf16[2,64,1536]{2,1,0:T(8,128)(2,1)}, u32[]{:S(2)}) copy-start(bf16[2,64,1536]{2,1,0:T(8,128)(2,1)} %param.10) | copy-start | bytes 1179652
  6.5 4.2 %copy-start.23 = (s32[16,4,1,2]{0,3,2,1:T(2,128)S(1)}, s32[16,4,1,2]{0,3,2,1:T(2,128)}, u32[]{:S(2)}) copy-start(s32[16,4,1,2]{0,3,2,1:T(2,128)} %param.13) | copy-start | bytes 1540
  6.5 60.5 %reduce-scatter.16.cloned.1.call-start = ((), (), s32[]{:S(2)}) async-start(), calls=%async_computation.5 | async-start | bytes 163840
  11.1 6.1 %copy-start.21 = (pred[16,8]{1,0:T(8,128)(4,1)}, pred[16,8]{1,0:T(8,128)(4,1)S(1)}, u32[]{:S(2)}) copy-start(pred[16,8]{1,0:T(8,128)(4,1)S(1)} %copy.20) | copy-start | bytes 388
  13.3 3.8 %copy-start.1 = (bf16[1,1024,4,1,128]{4,2,3,1,0:T(4,128)(2,1)}, bf16[1,1024,4,1,128]{4,2,3,1,0:T(4,128)(2,1)S(1)}, u32[]{:S(2)}) copy-start(bf16[1,1024,4,1,128]{4,2,3,1,0:T(4,128)(2,1)S(1)} %get-tuple-element.8) | copy-start | bytes 3145732
  13.3 3.8 %copy-start.3 = (bf16[1,1024,4,1,128]{4,2,3,1,0:T(4,128)(2,1)}, bf16[1,1024,4,1,128]{4,2,3,1,0:T(4,128)(2,1)S(1)}, u32[]{:S(2)}) copy-start(bf16[1,1024,4,1,128]{4,2,3,1,0:T(4,128)(2,1)S(1)} %get-tuple-element.9) | copy-start | bytes 3145732
  37.5 9.7 %copy-start.5 = (bf16[3,64,1024]{1,2,0:T(8,128)(2,1)}, bf16[3,64,1024]{1,2,0:T(8,128)(2,1)S(1)}, u32[]{:S(2)}) copy-start(bf16[3,64,1024]{1,2,0:T(8,128)(2,1)S(1)} %all_gather.15) | copy-start | bytes 1179652
  47.1 60.1 %reduce-scatter.18.cloned.1.call-start = ((), (), s32[]{:S(2)}) async-start(), calls=%async_computation.6 | async-start | bytes 163840
  67.0 19.4 %copy-start.4 = (bf16[1,1024,4,1,128]{4,2,3,1,0:T(4,128)(2,1)S(1)}, bf16[1,1024,4,1,128]{4,2,3,1,0:T(4,128)(2,1)}, u32[]{:S(2)}) copy-start(bf16[1,1024,4,1,128]{4,2,3,1,0:T(4,128)(2,1)} %copy-done.3) | copy-start | bytes 3145732
  85.8 0.6 copy-start.12
  90.4 54.2 %reduce-scatter.20.cloned.1.call-start = ((), (), s32[]{:S(2)}) async-start(), calls=%async_computation.7 | async-start | bytes 163840
  107.2 6.8 %copy-start.6 = (bf16[2,64,1536]{2,1,0:T(8,128)(2,1)S(1)}, bf16[2,64,1536]{2,1,0:T(8,128)(2,1)}, u32[]{:S(2)}) copy-start(bf16[2,64,1536]{2,1,0:T(8,128)(2,1)} %param.9) | copy-start | bytes 1179652
  107.2 18.7 %copy-start.9 = (pred[1024,512]{1,0:T(32,128)(4,1)S(1)}, pred[1024,512]{1,0:T(32,128)(4,1)}, u32[]{:S(2)}) copy-start(pred[1024,512]{1,0:T(32,128)(4,1)} %broadcast_in_dim.38) | copy-start | bytes 1572868
  114.0 12.6 %copy-start.13 = (bf16[64,1024]{1,0:T(8,128)(2,1)S(1)}, bf16[64,1024]{1,0:T(8,128)(2,1)}, u32[]{:S(2)}) copy-start(bf16[64,1024]{1,0:T(8,128)(2,1)} %copy-done.12) | copy-start | bytes 393220
  116.7 9.8 %copy-start.15 = (f32[64,512]{1,0:T(8,128)S(1)}, f32[64,512]{1,0:T(8,128)}, u32[]{:S(2)}) copy-start(f32[64,512]{1,0:T(8,128)} %fusion.40) | copy-start | bytes 393220
  125.9 0.7 copy-start.16
  125.9 1.8 copy-start.22
  127.6 57.0 %reduce-scatter.22.cloned.1.call-start = ((), (), s32[]{:S(2)}) async-start(), calls=%async_computation.8 | async-start | bytes 163840
  152.0 12.7 %copy-start.2 = (bf16[1,1024,4,1,128]{4,2,3,1,0:T(4,128)(2,1)S(1)}, bf16[1,1024,4,1,128]{4,2,3,1,0:T(4,128)(2,1)}, u32[]{:S(2)}) copy-start(bf16[1,1024,4,1,128]{4,2,3,1,0:T(4,128)(2,1)} %copy-done.1) | copy-start | bytes 3145732
  152.9 11.4 %copy-start.17 = (bf16[64,1024]{1,0:T(8,128)(2,1)S(1)}, bf16[64,1024]{1,0:T(8,128)(2,1)}, u32[]{:S(2)}) copy-start(bf16[64,1024]{1,0:T(8,128)(2,1)} %copy-done.16) | copy-start | bytes 393220
  152.9 11.7 %copy-start.7 = (pred[1024,512]{1,0:T(32,128)(4,1)S(1)}, pred[1024,512]{1,0:T(32,128)(4,1)}, u32[]{:S(2)}) copy-start(pred[1024,512]{1,0:T(32,128)(4,1)} %broadcast_in_dim.39) | copy-start | bytes 1572868
  152.9 11.7 %copy-start.10 = (pred[1024,512]{1,0:T(32,128)(4,1)S(1)}, pred[1024,512]{1,0:T(32,128)(4,1)}, u32[]{:S(2)}) copy-start(pred[1024,512]{1,0:T(32,128)(4,1)} %broadcast_in_dim.40) | copy-start | bytes 1572868
  152.9 11.7 %copy-start.14 = (bf16[64,1024]{1,0:T(8,128)(2,1)S(1)}, bf16[64,1024]{1,0:T(8,128)(2,1)}, u32[]{:S(2)}) copy-start(bf16[64,1024]{1,0:T(8,128)(2,1)} %copy-done.12) | copy-start | bytes 393220
  162.1 0.7 copy-start.19
  167.8 56.2 %reduce-scatter.24.cloned.1.call-start = ((), (), s32[]{:S(2)}) async-start(), calls=%async_computation.9 | async-start | bytes 163840
  194.1 11.0 %copy-start.20 = (bf16[64,1024]{1,0:T(8,128)(2,1)S(1)}, bf16[64,1024]{1,0:T(8,128)(2,1)}, u32[]{:S(2)}) copy-start(bf16[64,1024]{1,0:T(8,128)(2,1)} %copy-done.19) | copy-start | bytes 393220
  194.1 11.3 %copy-start.8 = (pred[1024,512]{1,0:T(32,128)(4,1)S(1)}, pred[1024,512]{1,0:T(32,128)(4,1)}, u32[]{:S(2)}) copy-start(pred[1024,512]{1,0:T(32,128)(4,1)} %broadcast_in_dim.39) | copy-start | bytes 1572868
  194.2 11.3 %copy-start.11 = (pred[1024,512]{1,0:T(32,128)(4,1)S(1)}, pred[1024,512]{1,0:T(32,128)(4,1)}, u32[]{:S(2)}) copy-start(pred[1024,512]{1,0:T(32,128)(4,1)} %broadcast_in_dim.40) | copy-start | bytes 1572868
  194.2 11.3 %copy-start.18 = (bf16[64,1024]{1,0:T(8,128)(2,1)S(1)}, bf16[64,1024]{1,0:T(8,128)(2,1)}, u32[]{:S(2)}) copy-start(bf16[64,1024]{1,0:T(8,128)(2,1)} %copy-done.16) | copy-start | bytes 393220
Sparse Core Ops, SparseCore 0:
  47.3 19.7 reduce-scatter.15
  90.5 16.6 reduce-scatter.17
  127.7 16.7 reduce-scatter.19
  167.9 16.6 reduce-scatter.21
  207.3 16.6 reduce-scatter.23
where the time goes:
time: 238 us; the launch traced here: 237 us
  waiting for transfers between devices  68.4 us (29%)
  matrix products  57.8 us (24%)
  blocking collectives  48.8 us (21%)
  local copies, waits for them, and re-layouts  41.5 us (17%)
  between operations  13.5 us (6%)
  other arithmetic  6.91 us (3%)
    unnamed x10, waiting for transfers between devices  68.4 us
    all_gather x4, blocking collectives, per_device(): newest = lax.all_gather(latest, 'src', axis=1, tiled=True)  36.9 us
    dot_general x5, matrix products, per_device(): jnp.einsum('ceb,cbd->ced', residual_field, near_inverse, preferred_elemen...  33.3 us
    dot_general x15, matrix products, couple(): jnp.dot(columns, matrices[delay - 1], preferred_element_type=jnp.float32)  16.1 us
    all_gather x1, blocking collectives, per_device(): gathered = lax.all_gather(stacked, 'src', axis=2, tiled=True)  11.9 us
    broadcast_in_dim x6, local copies, waits for them, and re-layouts, per_device(): combined = jnp.where(chosen, kernel[tap_index], combined)  11.4 us
    select_n x3, local copies, waits for them, and re-layouts, per_device(): combined = jnp.where(chosen, kernel[tap_index], combined)  10.7 us
    dot_general x7, matrix products, project(): jnp.einsum('ceb,crb->ecr', current, proj_basis, preferred_element_type=jn...  8.37 us
  transfers between devices with their start and end apart: 5, of which 5 were waited for; matrix products, arithmetic and copies ran while one was open for 8% of the time, Pallas kernels for 0%

commit v1 on v0

--- a/solution.py
+++ b/solution.py
@@ -43,7 +43,8 @@
     latest = None
     for step in range(STEPS):
         if step > 0:
-            newest = lax.all_gather(latest, "src", axis=1, tiled=True)
+            parts = lax.all_gather(latest, "src")
+            newest = jnp.concatenate(parts, axis=1)
             past = past[1:] + [newest]
         partial_value = couple(past[-1], 1) + couple(past[-2], 2) + couple(past[-3], 3)
         field = lax.psum_scatter(

time: 238 us -> 243 us (1.021)
  waiting for transfers between devices: 68.4 us -> 81.5 us
  local copies, waits for them, and re-layouts: 41.5 us -> 31.5 us
  matrix products: 57.8 us -> 61.4 us
  other arithmetic: 6.91 us -> 4.07 us
    unnamed x10, waiting for transfers between devices: 68.4 us -> 81.5 us
    broadcast_in_dim x6 -> x0, local copies, waits for them, and re-layouts: 11.4 us -> none  [per_device(): combined = jnp.where(chosen, kernel[tap_index], combined)]
    reshape x4 -> x0, local copies, waits for them, and re-layouts: 3.48 us -> none  [project(): return projected.astype(jnp.bfloat16).reshape(excite, local_clusters * rank)]
    another operation x0 -> x4, local copies, waits for them, and re-layouts: none -> 3.39 us  [per_device(): parts = lax.all_gather(latest, 'src')]
    select_n x2 -> x1, other arithmetic: 6.87 us -> 4.03 us  [per_device(): combined = jnp.where(chosen, kernel[tap_index], combined)]
    unnamed x53 -> x21, local copies, waits for them, and re-layouts: 6.97 us -> 9.12 us
  transfers between devices with their start and end apart: 5 -> 5, of which waited for: 5 -> 5; matrix products, arithmetic and copies ran while one was open for 8% -> 2% of each run, Pallas kernels for 0% -> 0%
where the time goes in v1:
time: 243 us; the launch traced here: 242 us
  waiting for transfers between devices  81.5 us (34%)
  matrix products  61.4 us (25%)
  blocking collectives  50.1 us (21%)
  local copies, waits for them, and re-layouts  31.5 us (13%)
  between operations  13.4 us (6%)
  other arithmetic  4.07 us (2%)
    unnamed x10, waiting for transfers between devices  81.5 us
    all_gather x4, blocking collectives, per_device(): parts = lax.all_gather(latest, 'src')  37.1 us
    dot_general x5, matrix products, per_device(): jnp.einsum('ceb,cbd->ced', residual_field, near_inverse, preferred_elemen...  33.3 us
    dot_general x15, matrix products, couple(): jnp.dot(columns, matrices[delay - 1], preferred_element_type=jnp.float32)  18.4 us
    all_gather x1, blocking collectives, per_device(): gathered = lax.all_gather(stacked, 'src', axis=2, tiled=True)  13 us
    dot_general x7, matrix products, project(): jnp.einsum('ceb,crb->ecr', current, proj_basis, preferred_element_type=jn...  9.65 us
    select_n x3, local copies, waits for them, and re-layouts, per_device(): combined = jnp.where(chosen, kernel[tap_index], combined)  9.58 us
    unnamed x21, local copies, waits for them, and re-layouts  9.12 us
  transfers between devices with their start and end apart: 5, of which 5 were waited for; matrix products, arithmetic and copies ran while one was open for 2% of the time, Pallas kernels for 0%

profile of v1, /device:TPU:0, one launch (start us, length us, event | category | flops | bytes accessed | tf_op | source)
XLA Modules:
  0.0 242.1 jit_solution(6981661725050741938)
XLA Ops:
  6.5 1.5 convolution_convert_fusion.11
  8.1 1.4 convolution_convert_fusion.9
  9.4 1.4 convolution_convert_fusion.10
  11.2 13.0 %all_gather.15 = bf16[3,64,1024]{1,2,0:T(8,128)(2,1)} all-gather(bf16[3,64,128]{1,2,0:T(8,128)(2,1)S(1)} %pad_maximum_fusion), channel_id=1, replica_groups=mesh['obs'=4,'src'=8] {'src'}, dimensions={2}, use_global_device_ids=true | all-gather | bytes 442368 | tf_op jit(solution)/shard_map/all_gather | solution.py:40
  24.1 1.7 fusion.64
  25.8 3.0 %squeeze.38 = bf16[16,64,8,64]{3,2,1,0:T(8,128)(2,1)S(1)} reshape(bf16[1,1024,4,1,128]{4,2,3,1,0:T(4,128)(2,1)} %get-tuple-element.8) | data formatting | bytes 2097152 | tf_op jit(solution)/shard_map/squeeze | solution.py:27
  28.9 1.9 squeeze.36
  30.7 4.0 %select_select_fusion = (bf16[16,64,8,64]{3,2,1,0:T(8,128)(2,1)}, bf16[16,64,8,64]{3,2,1,0:T(8,128)(2,1)}, bf16[16,64,8,64]{3,2,1,0:T(8,128)(2,1)}) fusion(bf16[16,64,8,64]{3,2,1,0:T(8,128)(2,1)S(1)} %squeeze.38, bf16[16,64,8,64]{3,2,1,0:T(8,128)(2,1)} %squeeze.36, pred[16,8]{1,0:T(8,128)(4,1)S(1)} %copy.24, pred[16,8]{1,0:T(8,128)(4,1)S(1)} %copy.23, ...), kind=kLoop, calls=%fused_computation.17 | loop fusion | flops 2621440 | bytes 5243264 | tf_op jit(solution)/shard_map/jit(_where)/select_n | solution.py:27
  34.8 3.2 %select_n.149 = bf16[1024,512]{1,0:T(8,128)(2,1)S(1)} reshape(bf16[16,64,8,64]{3,2,1,0:T(8,128)(2,1)} %get-tuple-element.5) | data formatting | bytes 2097152 | tf_op jit(solution)/shard_map/jit(_where)/select_n | solution.py:27
  38.0 3.2 %select_n.146 = bf16[1024,512]{1,0:T(8,128)(2,1)S(1)} reshape(bf16[16,64,8,64]{3,2,1,0:T(8,128)(2,1)} %get-tuple-element.6) | data formatting | bytes 2097152 | tf_op jit(solution)/shard_map/jit(_where)/select_n | solution.py:27
  41.2 3.2 %select_n.143 = bf16[1024,512]{1,0:T(8,128)(2,1)S(1)} reshape(bf16[16,64,8,64]{3,2,1,0:T(8,128)(2,1)} %get-tuple-element.7) | data formatting | bytes 2097152 | tf_op jit(solution)/shard_map/jit(_where)/select_n | solution.py:27
  44.4 1.3 fusion.42
  45.6 1.3 convolution_add_fusion.7
  46.9 1.9 fusion.11
  48.8 1.6 copy.38
  50.5 1.9 fusion.39
  52.4 1.9 fusion.41
  54.3 16.0 %reduce-scatter.16.cloned.1.call-done = bf16[128,64]{1,0:T(8,128)(2,1)} async-done(((bf16[512,64]{1,0:T(8,128)(2,1)}), bf16[128,64]{1,0:T(8,128)(2,1)}) %reduce-scatter.16.cloned.1.call-update) | async-done | bytes 16400
  70.3 6.7 %bitcast_dynamic-update-slice_fusion.3 = (bf16[5,2,64,1536]{3,2,1,0:T(8,128)(2,1)}, bf16[2,64,1536]{2,1,0:T(8,128)(2,1)}) fusion(bf16[2,1536,1536]{2,1,0:T(8,128)(2,1)} %param.11, bf16[64,2,64]{0,2,1:T(8,128)(2,1)} %bitcast.228, bf16[2,64,1536]{2,1,0:T(8,128)(2,1)S(1)} %copy-done, bf16[5,2,64,1536]{3,2,1,0:T(8,128)(2,1)} %param.8), kind=kOutput, calls=%fused_computation.59 | convolution fusion | flops 629932032 | bytes 11042816 | tf_op jit(solution)/shard_map/ceb,cbd->ced/dot_general | solution.py:58
  76.9 1.4 fusion.14
  78.9 0.8 all_gather_reshape.12
  79.8 9.2 %all_gather.16 = bf16[8,64,128]{2,1,0:T(8,128)(2,1)S(1)} all-gather(bf16[1,64,128]{2,1,0:T(8,128)(2,1)S(1)} %all_gather_reshape.12), channel_id=1, replica_groups=mesh['obs'=4,'src'=8] {'src'}, dimensions={0}, use_global_device_ids=true | all-gather | bytes 147456 | tf_op jit(solution)/shard_map/all_gather | solution.py:46
  89.6 1.9 fusion.13
  91.5 1.6 copy.40
  93.2 1.9 fusion.40
  95.1 14.9 %reduce-scatter.18.cloned.1.call-done = bf16[128,64]{1,0:T(8,128)(2,1)} async-done(((bf16[512,64]{1,0:T(8,128)(2,1)}), bf16[128,64]{1,0:T(8,128)(2,1)}) %reduce-scatter.18.cloned.1.call-update) | async-done | bytes 16400
  110.0 6.7 %bitcast_dynamic-update-slice_fusion.2 = (bf16[5,2,64,1536]{3,2,1,0:T(8,128)(2,1)}, bf16[2,64,1536]{2,1,0:T(8,128)(2,1)}) fusion(bf16[5,2,64,1536]{3,2,1,0:T(8,128)(2,1)} %get-tuple-element.13, bf16[2,1536,1536]{2,1,0:T(8,128)(2,1)} %param.11, bf16[64,2,64]{0,2,1:T(8,128)(2,1)} %bitcast.227, bf16[2,64,1536]{2,1,0:T(8,128)(2,1)S(1)} %copy-done, ...), kind=kOutput, calls=%fused_computation.58 | convolution fusion | flops 629932032 | bytes 11042816 | tf_op jit(solution)/shard_map/ceb,cbd->ced/dot_general | solution.py:58
  116.7 1.4 fusion.15
  118.7 0.8 all_gather_reshape.13
  119.5 9.3 %all_gather.17 = bf16[8,64,128]{2,1,0:T(8,128)(2,1)S(1)} all-gather(bf16[1,64,128]{2,1,0:T(8,128)(2,1)S(1)} %all_gather_reshape.13), channel_id=1, replica_groups=mesh['obs'=4,'src'=8] {'src'}, dimensions={0}, use_global_device_ids=true | all-gather | bytes 147456 | tf_op jit(solution)/shard_map/all_gather | solution.py:46
  129.8 1.9 fusion.12
  131.7 1.6 copy.42
  133.4 16.8 %reduce-scatter.20.cloned.1.call-done = bf16[128,64]{1,0:T(8,128)(2,1)} async-done(((bf16[512,64]{1,0:T(8,128)(2,1)}), bf16[128,64]{1,0:T(8,128)(2,1)}) %reduce-scatter.20.cloned.1.call-update) | async-done | bytes 16400
  150.2 6.7 %bitcast_dynamic-update-slice_fusion.1 = (bf16[5,2,64,1536]{3,2,1,0:T(8,128)(2,1)}, bf16[2,64,1536]{2,1,0:T(8,128)(2,1)}) fusion(bf16[5,2,64,1536]{3,2,1,0:T(8,128)(2,1)} %get-tuple-element.15, bf16[2,1536,1536]{2,1,0:T(8,128)(2,1)} %param.11, bf16[64,2,64]{0,2,1:T(8,128)(2,1)} %bitcast.229, bf16[2,64,1536]{2,1,0:T(8,128)(2,1)S(1)} %copy-done, ...), kind=kOutput, calls=%fused_computation.57 | convolution fusion | flops 629932032 | bytes 11042816 | tf_op jit(solution)/shard_map/ceb,cbd->ced/dot_general | solution.py:58
  156.9 1.4 fusion.16
  158.9 0.8 all_gather_reshape.14
  159.8 9.3 %all_gather.18 = bf16[8,64,128]{2,1,0:T(8,128)(2,1)S(1)} all-gather(bf16[1,64,128]{2,1,0:T(8,128)(2,1)S(1)} %all_gather_reshape.14), channel_id=1, replica_groups=mesh['obs'=4,'src'=8] {'src'}, dimensions={0}, use_global_device_ids=true | all-gather | bytes 147456 | tf_op jit(solution)/shard_map/all_gather | solution.py:46
  170.0 1.2 convolution_add_fusion.3
  171.3 0.9 fusion.9
  172.2 1.6 copy.44
  173.9 16.8 %reduce-scatter.22.cloned.1.call-done = bf16[128,64]{1,0:T(8,128)(2,1)} async-done(((bf16[512,64]{1,0:T(8,128)(2,1)}), bf16[128,64]{1,0:T(8,128)(2,1)}) %reduce-scatter.22.cloned.1.call-update) | async-done | bytes 16400
  190.7 6.7 %bitcast_dynamic-update-slice_fusion = (bf16[5,2,64,1536]{3,2,1,0:T(8,128)(2,1)}, bf16[2,64,1536]{2,1,0:T(8,128)(2,1)}) fusion(bf16[5,2,64,1536]{3,2,1,0:T(8,128)(2,1)} %get-tuple-element.17, bf16[2,1536,1536]{2,1,0:T(8,128)(2,1)} %param.11, bf16[64,2,64]{0,2,1:T(8,128)(2,1)} %bitcast.230, bf16[2,64,1536]{2,1,0:T(8,128)(2,1)S(1)} %copy-done, ...), kind=kOutput, calls=%fused_computation.56 | convolution fusion | flops 629932032 | bytes 11042816 | tf_op jit(solution)/shard_map/ceb,cbd->ced/dot_general | solution.py:58
  197.4 1.4 fusion.17
  199.4 0.8 all_gather_reshape.15
  200.2 9.3 %all_gather.19 = bf16[8,64,128]{2,1,0:T(8,128)(2,1)S(1)} all-gather(bf16[1,64,128]{2,1,0:T(8,128)(2,1)S(1)} %all_gather_reshape.15), channel_id=1, replica_groups=mesh['obs'=4,'src'=8] {'src'}, dimensions={0}, use_global_device_ids=true | all-gather | bytes 147456 | tf_op jit(solution)/shard_map/all_gather | solution.py:46
  209.8 1.2 convolution_add_fusion.1
  212.1 16.9 %reduce-scatter.24.cloned.1.call-done = bf16[128,64]{1,0:T(8,128)(2,1)} async-done(((bf16[512,64]{1,0:T(8,128)(2,1)}), bf16[128,64]{1,0:T(8,128)(2,1)}) %reduce-scatter.24.cloned.1.call-update) | async-done | bytes 16400
  229.0 6.6 %fusion.6 = bf16[5,2,64,1536]{3,2,1,0:T(8,128)(2,1)} fusion(bf16[5,2,64,1536]{3,2,1,0:T(8,128)(2,1)} %get-tuple-element.19, bf16[2,1536,1536]{2,1,0:T(8,128)(2,1)} %param.11, bf16[64,2,64]{0,2,1:T(8,128)(2,1)} %bitcast.231, bf16[2,64,1536]{2,1,0:T(8,128)(2,1)S(1)} %copy-done, bf16[5,2,64,1536]{3,2,1,0:T(8,128)(2,1)} %param.8), kind=kOutput, calls=%fused_computation.16 | convolution fusion | flops 629932032 | bytes 10649600 | tf_op jit(solution)/shard_map/ceb,cbd->ced/dot_general | solution.py:58
  (43 shorter events, 7.0 us)
Async XLA Ops:
  6.5 63.7 %copy-start = (bf16[2,64,1536]{2,1,0:T(8,128)(2,1)S(1)}, bf16[2,64,1536]{2,1,0:T(8,128)(2,1)}, u32[]{:S(2)}) copy-start(bf16[2,64,1536]{2,1,0:T(8,128)(2,1)} %param.10) | copy-start | bytes 1179652
  6.5 4.3 %copy-start.7 = (s32[16,4,1,2]{0,3,2,1:T(2,128)S(1)}, s32[16,4,1,2]{0,3,2,1:T(2,128)}, u32[]{:S(2)}) copy-start(s32[16,4,1,2]{0,3,2,1:T(2,128)} %param.13) | copy-start | bytes 1540
  6.5 17.6 %copy-start.1 = (bf16[2,1024,4,1,128]{4,2,3,1,0:T(4,128)(2,1)S(1)}, bf16[2,1024,4,1,128]{4,2,3,1,0:T(4,128)(2,1)}, u32[]{:S(2)}) copy-start(bf16[2,1024,4,1,128]{4,2,3,1,0:T(4,128)(2,1)} %param.12) | copy-start | bytes 6291460
  6.5 63.7 %reduce-scatter.16.cloned.1.call-start = ((), (), s32[]{:S(2)}) async-start(), calls=%async_computation.5 | async-start | bytes 163840
  50.4 59.6 %reduce-scatter.18.cloned.1.call-start = ((), (), s32[]{:S(2)}) async-start(), calls=%async_computation.6 | async-start | bytes 163840
  89.0 0.6 copy-start.2
  93.1 57.1 %reduce-scatter.20.cloned.1.call-start = ((), (), s32[]{:S(2)}) async-start(), calls=%async_computation.7 | async-start | bytes 163840
  128.9 0.6 copy-start.4
  133.3 57.3 %reduce-scatter.22.cloned.1.call-start = ((), (), s32[]{:S(2)}) async-start(), calls=%async_computation.8 | async-start | bytes 163840
  159.8 11.5 %copy-start.3 = (bf16[8,64,128]{2,1,0:T(8,128)(2,1)S(1)}, bf16[8,64,128]{2,1,0:T(8,128)(2,1)}, u32[]{:S(2)}) copy-start(bf16[8,64,128]{2,1,0:T(8,128)(2,1)} %copy-done.2) | copy-start | bytes 393220
  169.1 0.7 copy-start.6
  173.8 55.2 %reduce-scatter.24.cloned.1.call-start = ((), (), s32[]{:S(2)}) async-start(), calls=%async_computation.9 | async-start | bytes 163840
  200.2 10.8 %copy-start.5 = (bf16[8,64,128]{2,1,0:T(8,128)(2,1)S(1)}, bf16[8,64,128]{2,1,0:T(8,128)(2,1)}, u32[]{:S(2)}) copy-start(bf16[8,64,128]{2,1,0:T(8,128)(2,1)} %copy-done.4) | copy-start | bytes 393220
Sparse Core Ops, SparseCore 0:
  50.5 19.6 reduce-scatter.15
  93.2 16.7 reduce-scatter.17
  133.5 16.7 reduce-scatter.19
  173.9 16.7 reduce-scatter.21
  212.3 16.6 reduce-scatter.23
